TPU v7x, 32 devices: a whole 2x2x4 slice. The times are simulated.
32 devices in a mesh: member: 4 (over y, x), grid: 8 (over z, core).
Axes of the slice: x: 2, y: 2, z: 4, core: 2. Of those that a mesh axis runs over, the one named last changes fastest.
Arguments:
- latent: bfloat16 [4, 16384, 1024], P('member', 'grid'), may hold values from -6 to 6
- w_in: bfloat16 [1024, 1024], P(('member', 'grid')), may hold values from -0.1875 to 0.1875
- b_in: float32 [1024], replicated, may hold values from -3 to 3
- w_out: bfloat16 [100, 1024], replicated, may hold values from -0.1875 to 0.1875
- b_out: float32 [100], replicated, may hold values from -3 to 3
- targets: float32 [100, 16384], P(None, 'grid'), may hold values from -6 to 6
- var_weight: float32 [100], replicated, may hold values from 0.5 to 5
- plan: int32 [3, 4], replicated, may hold values from 0 to 3, as said below
Outputs:
- loss: float32 [], replicated
- grad_latent: bfloat16 [4, 16384, 1024], P('member', 'grid')
- grad_w_in: float32 [1024, 1024], P(('member', 'grid'))
- grad_b_in: float32 [1024], replicated
- grad_w_out: float32 [100, 1024], replicated
- grad_b_out: float32 [100], replicated
Inputs may be any that keep to these rules, and one draw needn't show every extreme that they name: `plan`: each row is a perfect pairing of the 4 members: no member is its own partner, the partner of a member's partner is the member, and no pair occurs in two rows.
All inputs are finite; a program needn't handle non-finite values.
Results may differ from a plain program's by a relative error of at most 0.0095.
Values may be sent and summed in bfloat16 or wider, within the bound.
A program may use at most 128 MiB of HBM per device.

v0:
```python
import jax
import jax.numpy as jnp
from jax import lax
from jax.sharding import PartitionSpec as P

DELTA = 0.25


def make_fold(mine, partner_rows):

    def fold(carry, piece, start):
        count = piece.shape[0]
        labels = jnp.arange(count, dtype=jnp.int32)
        weights = jnp.sum((partner_rows[:, None] == labels[None, :]).astype(jnp.float32), axis=0)
        diff = mine[None] - piece
        root = jnp.sqrt(diff * diff + DELTA * DELTA)
        slope_sum = jnp.einsum("k,kvp->vp", weights, diff / root)
        spread_sum = jnp.einsum("k,kvp->vp", weights, root - DELTA)
        return (slope_sum, spread_sum)

    return fold


def shards(latent, w_in, b_in, w_out, b_out, targets, var_weight, plan):
    hidden_in = latent[0]
    points = hidden_in.shape[0]
    rounds = plan.shape[0]
    w_full = lax.all_gather(w_in, ("member", "grid"), axis=0, tiled=True)
    member = lax.axis_index("member")
    grid_index = lax.axis_index("grid")
    members = lax.axis_size("member")
    grid_count = lax.axis_size("grid")
    total = points * grid_count
    place = (grid_index * points + jnp.arange(points, dtype=jnp.int32)).astype(jnp.float32)
    area = jnp.cos(1.4 * (place + 0.5) / total)
    scale_map = area[None, :] * var_weight[:, None]
    partner_rows = lax.dynamic_index_in_dim(plan, member, 1, keepdims=False)
    pre = jnp.dot(hidden_in, w_full, preferred_element_type=jnp.float32) + b_in[None, :]
    act = jax.nn.gelu(pre).astype(jnp.bfloat16)
    field = jnp.dot(w_out, act.T, preferred_element_type=jnp.float32) + b_out[:, None]
    pre, act, field = (pre, act, field)
    fold_all = make_fold(field, partner_rows)
    slope_sum, spread_sum = fold_all(
        (
            jnp.zeros((w_out.shape[0], points), jnp.float32),
            jnp.zeros((w_out.shape[0], points), jnp.float32),
        ),
        lax.all_gather(field[None], "member", axis=0, tiled=True),
        jnp.int32(0),
    )
    miss = field - targets
    miss_root = jnp.sqrt(miss * miss + DELTA * DELTA)
    cot = scale_map * (miss / miss_root - slope_sum / rounds)
    terms = scale_map * (miss_root - DELTA - spread_sum / (2.0 * rounds))
    cot_b = cot.astype(jnp.bfloat16)
    dact = jnp.dot(cot_b.T, w_out, preferred_element_type=jnp.float32)
    _, pull = jax.vjp(jax.nn.gelu, pre)
    dpre = pull(dact)[0]
    dpre_b = dpre.astype(jnp.bfloat16)
    grad_hidden = jnp.dot(dpre_b, w_full.T, preferred_element_type=jnp.float32).astype(jnp.bfloat16)
    kappa = 4.0 / jnp.sqrt(jnp.float32(members * total))
    out_term = jnp.dot(cot_b, act, preferred_element_type=jnp.float32)
    sum_w2, sum_b2, sum_b1, sum_loss = lax.psum(
        (out_term, jnp.sum(cot, axis=1), jnp.sum(dpre, axis=0), jnp.sum(terms)), ("member", "grid")
    )
    row_count = w_in.shape[0]
    full_term = jnp.dot(hidden_in.T, dpre_b, preferred_element_type=jnp.float32)
    summed = lax.psum(full_term, ("member", "grid"))
    offset = (member * grid_count + grid_index) * row_count
    own_rows = lax.dynamic_slice_in_dim(summed, offset, row_count, 0)
    loss = sum_loss / (members * total * w_out.shape[0])
    return (
        loss,
        grad_hidden[None],
        own_rows * kappa,
        sum_b1 * kappa,
        sum_w2 * kappa,
        sum_b2 * kappa,
    )


def solution(mesh):
    placed = (
        P("member", "grid", None),
        P(("member", "grid"), None),
        P(),
        P(),
        P(),
        P(None, "grid"),
        P(),
        P(),
    )
    return jax.shard_map(
        shards,
        mesh=mesh,
        in_specs=placed,
        out_specs=(P(), P("member", "grid", None), P(("member", "grid"), None), P(), P(), P()),
        check_vma=False,
    )
```

profile of v0, /device:TPU:0, one launch (start us, length us, event | category | flops | bytes accessed | tf_op | source)
XLA Modules:
  0.0 314.8 jit_solution(176312685876041185)
XLA Ops:
  7.2 0.0 copy-start
  7.2 0.0 all-gather.5.cloned.1.call-start
  7.2 0.7 all-gather.5.cloned.1.call-update
  7.9 0.0 copy-start.5
  7.9 0.0 all-gather.7.cloned.1.call-start
  8.0 62.1 %all-gather.5.cloned.1.call-done = bf16[1024,1024]{1,0:T(8,128)(2,1)} async-done(((bf16[32,1024]{1,0:T(8,128)(2,1)}), bf16[1024,1024]{1,0:T(8,128)(2,1)}) %all-gather.5.cloned.1.call-update) | async-done | bytes 2097168 | tf_op jit(solution)/shard_map/all_gather | solution.py:28
  70.1 12.6 %multiply_convert_fusion = (bf16[2048,1024]{1,0:T(8,128)(2,1)S(1)}, f32[2048,1024]{1,0:T(8,128)}) fusion(f32[1024]{0:T(1024)} %param.10, bf16[1024,1024]{1,0:T(8,128)(2,1)} %all-gather.5.cloned.1.call-done, bf16[1,2048,1024]{2,1,0:T(8,128)(2,1)} %param.8), kind=kOutput, calls=%fused_computation.8 | convolution fusion | flops 4315938816 | bytes 18878464 | tf_op jit(solution)/shard_map/dot_general | solution.py:38
  82.7 0.0 copy-start.1
  82.7 0.0 copy-start.6
  82.7 2.0 copy-done.1
  84.7 0.0 copy-done
  84.8 0.0 copy-done.5
  84.8 2.4 convolution_add_fusion
  87.1 0.0 all-gather.7.cloned.1.call-update
  87.1 0.2 all-reduce.4.cloned.1.call-start
  87.4 0.0 copy-done.6
  87.4 0.2 dynamic-slice_reduce_fusion
  87.6 0.1 multiply_cosine_fusion
  87.6 0.1 convert_reduce_fusion
  87.7 44.5 %all-gather.7.cloned.1.call-done = f32[4,100,2048]{2,1,0:T(8,128)} async-done(((f32[1,100,2048]{2,1,0:T(8,128)}), f32[4,100,2048]{2,1,0:T(8,128)}) %all-gather.7.cloned.1.call-update) | async-done | bytes 3276816 | tf_op jit(solution)/shard_map/all_gather | solution.py:48
  132.2 0.0 slice-start
  132.2 4.1 %fusion.10 = (bf16[4,100,2048]{2,1,0:T(8,128)(2,1)S(1)}, bf16[4,100,2048]{2,1,0:T(8,128)(2,1)S(1)}) fusion(f32[4,100,2048]{2,1,0:T(8,128)} %all-gather.7.cloned.1.call-done, f32[100,2048]{1,0:T(8,128)} %bitcast.49), kind=kLoop, calls=%fused_computation.15 | loop fusion | flops 5734400 | bytes 7372800 | tf_op jit(solution)/shard_map/div | solution.py:17
  136.3 0.0 copy-start.3
  136.3 0.0 copy-start.4
  136.3 0.0 copy-start.7
  136.3 1.3 fusion.12
  137.7 0.0 copy-start.2
  137.7 0.0 slice-start.1
  137.7 1.3 fusion.14
  139.0 0.0 copy-done.3
  139.0 0.0 copy-done.4
  139.0 0.0 copy-done.7
  139.0 0.0 copy-start.10
  139.1 1.9 fusion.29
  140.9 0.0 copy-done.2
  140.9 1.6 fusion.24
  142.5 0.0 slice-done
  142.5 0.0 slice-done.1
  142.5 0.0 copy-done.10
  142.5 0.0 copy-start.8
  142.5 7.0 %fusion.30 = (f32[1024]{0:T(1024)S(1)}, bf16[2048,1024]{1,0:T(8,128)(2,1)S(1)}) fusion(f32[2048,1024]{1,0:T(8,128)S(1)} %bitcast.51, f32[1024]{0:T(1024)S(1)} %copy-done.10, bf16[100,1024]{1,0:T(8,128)(2,1)S(1)} %copy-done, bf16[100,2048]{1,0:T(8,128)(2,1)S(1)} %get-tuple-element.30), kind=kOutput, calls=%fused_computation.47 | convolution fusion | flops 465566720 | bytes 13205504 | tf_op jit(solution)/shard_map/dot_general | solution.py:56
  149.5 0.0 copy-start.11
  149.5 2.0 copy-done.11
  151.5 0.0 copy-done.8
  151.5 6.2 %fusion.16 = f32[1024,1024]{0,1:T(8,128)} fusion(bf16[1,2048,1024]{2,1,0:T(8,128)(2,1)S(1)} %copy-done.8, bf16[2048,1024]{1,0:T(8,128)(2,1)S(1)} %get-tuple-element.37), kind=kOutput, calls=%fused_computation.22 | convolution fusion | flops 4294967296 | bytes 12582912 | tf_op jit(solution)/shard_map/dot_general | solution.py:67
  157.7 0.0 copy-start.9
  157.7 0.0 all-reduce.4.cloned.1.call-update
  157.7 40.3 %all-reduce = (f32[]{:T(128)}, f32[1024]{0:T(1024)S(1)}, f32[100]{0:T(128)S(1)}) all-reduce(f32[]{:T(128)} %get-tuple-element.33, f32[1024]{0:T(1024)S(1)} %get-tuple-element.36, f32[100]{0:T(128)S(1)} %get-tuple-element.29), channel_id=1, replica_groups=mesh['member'=4,'grid'=8] {'member','grid'}, use_global_device_ids=true, to_apply=%region_2.3 | all-reduce | flops 1125 | bytes 9000 | tf_op jit(solution)/shard_map/psum | solution.py:63
  198.7 0.5 broadcast_multiply_fusion.2
  199.2 0.6 broadcast_multiply_fusion.1
  199.8 0.0 copy-done.9
  199.8 8.3 %convert_bitcast_fusion = bf16[1,2048,1024]{2,1,0:T(8,128)(2,1)} fusion(bf16[1024,1024]{1,0:T(8,128)(2,1)S(1)} %copy-done.9, bf16[2048,1024]{1,0:T(8,128)(2,1)} %copy-done.11), kind=kOutput, calls=%fused_computation.13 | convolution fusion | flops 4297064448 | bytes 10485760 | tf_op jit(solution)/shard_map/dot_general | solution.py:60
  208.1 95.1 %all-reduce.4.cloned.1.call-done = (f32[1024,1024]{0,1:T(8,128)}, f32[100,1024]{1,0:T(8,128)}) async-done(((f32[1024,1024]{0,1:T(8,128)}, f32[100,1024]{1,0:T(8,128)}), (f32[1024,1024]{0,1:T(8,128)}, f32[100,1024]{1,0:T(8,128)})) %all-reduce.4.cloned.1.call-update) | async-done | bytes 4603920 | tf_op jit(solution)/shard_map/psum | solution.py:68
  303.2 1.2 dynamic-slice_multiply_fusion
  304.5 0.8 copy.16
  305.3 1.8 broadcast_multiply_fusion
  (1 shorter events, 0.0 us)
Async XLA Ops:
  7.2 77.6 %copy-start = (bf16[100,1024]{1,0:T(8,128)(2,1)S(1)}, bf16[100,1024]{1,0:T(8,128)(2,1)}, u32[]{:S(2)}) copy-start(bf16[100,1024]{1,0:T(8,128)(2,1)} %param.11) | copy-start | bytes 614404
  7.2 62.9 %all-gather.5.cloned.1.call-start = ((), (), s32[]{:S(2)}) async-start(), calls=%async_computation | async-start | bytes 2162688 | tf_op jit(solution)/shard_map/all_gather | solution.py:28
  7.9 76.8 %copy-start.5 = (f32[100]{0:T(128)S(1)}, f32[100]{0:T(128)}, u32[]{:S(2)}) copy-start(f32[100]{0:T(128)} %param.12) | copy-start | bytes 1204
  7.9 124.3 %all-gather.7.cloned.1.call-start = ((), (), s32[]{:S(2)}) async-start(), calls=%async_computation.1 | async-start | bytes 4259840 | tf_op jit(solution)/shard_map/all_gather | solution.py:48
  82.7 2.0 copy-start.1
  82.7 4.6 %copy-start.6 = (s32[3,4]{1,0:T(4,128)S(1)}, s32[3,4]{1,0:T(4,128)}, u32[]{:S(2)}) copy-start(s32[3,4]{1,0:T(4,128)} %param.15) | copy-start | bytes 148
  87.1 216.1 %all-reduce.4.cloned.1.call-start = ((), (), s32[]{:S(2)}) async-start(), calls=%async_computation.2 | async-start | bytes 9240576 | tf_op jit(solution)/shard_map/psum | solution.py:68
  132.2 10.3 %slice-start = ((s8[8388608]{0:T(1024)(128)(4,1)}), s8[4194304]{0:T(1024)(128)(4,1)S(1)}, s32[]{:S(2)}) async-start(s8[8388608]{0:T(1024)(128)(4,1)} %bitcast.50), calls=%async_computation.3 | async-start | bytes 8388608
  136.3 2.7 copy-start.3
  136.3 2.7 copy-start.4
  136.3 2.7 copy-start.7
  137.7 3.3 %copy-start.2 = (bf16[2048,1024]{1,0:T(8,128)(2,1)S(1)}, bf16[2048,1024]{1,0:T(8,128)(2,1)}, u32[]{:S(2)}) copy-start(bf16[2048,1024]{1,0:T(8,128)(2,1)} %copy-done.1) | copy-start | bytes 12582916
  137.7 4.8 %slice-start.1 = ((s8[8388608]{0:T(1024)(128)(4,1)}), s8[4194304]{0:T(1024)(128)(4,1)S(1)}, s32[]{:S(2)}) async-start(s8[8388608]{0:T(1024)(128)(4,1)} %bitcast.50), calls=%async_computation.4 | async-start | bytes 8388608
  139.0 3.4 %copy-start.10 = (f32[1024]{0:T(1024)S(1)}, f32[1024]{0:T(1024)}, u32[]{:S(2)}) copy-start(f32[1024]{0:T(1024)} %param.10) | copy-start | bytes 12292
  142.5 9.0 %copy-start.8 = (bf16[1,2048,1024]{2,1,0:T(8,128)(2,1)S(1)}, bf16[1,2048,1024]{2,1,0:T(8,128)(2,1)}, u32[]{:S(2)}) copy-start(bf16[1,2048,1024]{2,1,0:T(8,128)(2,1)} %param.8) | copy-start | bytes 12582916
  149.5 2.0 copy-start.11
  157.7 42.1 %copy-start.9 = (bf16[1024,1024]{1,0:T(8,128)(2,1)S(1)}, bf16[1024,1024]{1,0:T(8,128)(2,1)}, u32[]{:S(2)}) copy-start(bf16[1024,1024]{1,0:T(8,128)(2,1)} %all-gather.5.cloned.1.call-done) | copy-start | bytes 6291460
Sparse Core Ops, SparseCore 0:
  11.0 59.0 all-gather.4
  87.3 44.8 all-gather.6
  157.8 145.3 all-reduce.3
where the time goes:
time: 315 us
  waiting for transfers between devices  202 us (64%)
  matrix products  40.7 us (13%)
  blocking collectives  40.3 us (13%)
  between operations  15.7 us (5%)
  other arithmetic  10.2 us (3%)
  local copies, waits for them, and re-layouts  5.12 us (2%)
    psum x1, waiting for transfers between devices, shards(): summed = lax.psum(full_term, ('member', 'grid'))  95.1 us
    all_gather x1, waiting for transfers between devices, shards(): w_full = lax.all_gather(w_in, ('member', 'grid'), axis=0, tiled=True)  62.1 us
    all_gather x1, waiting for transfers between devices, shards(): lax.all_gather(field[None], 'member', axis=0, tiled=True)  44.5 us
    psum x1, blocking collectives, shards(): lax.psum((out_term, jnp.sum(cot, axis=1), jnp.sum(dpre, axis=0), jnp.sum(...  40.3 us
    dot_general x1, matrix products, shards(): jnp.dot(hidden_in, w_full, preferred_element_type=jnp.float32)  12.6 us
    dot_general x1, matrix products, shards(): jnp.dot(dpre_b, w_full.T, preferred_element_type=jnp.float32)  8.35 us
    dot_general x1, matrix products, shards(): dact = jnp.dot(cot_b.T, w_out, preferred_element_type=jnp.float32)  6.99 us
  transfers between devices with their start and end apart: 3, of which 3 were waited for; matrix products, arithmetic and copies ran while one was open for 3% of the time, Pallas kernels for 0%

commit v1 on v0

--- a/solution.py
+++ b/solution.py
@@ -22,6 +22,11 @@
 
 
 def shards(latent, w_in, b_in, w_out, b_out, targets, var_weight, plan):
+
+    def _direct_chains(my_tile):
+        now = lax.psum(my_tile, axis_name="grid")
+        return lax.psum(now, axis_name="member")
+
     hidden_in = latent[0]
     points = hidden_in.shape[0]
     rounds = plan.shape[0]
@@ -60,8 +65,8 @@
     grad_hidden = jnp.dot(dpre_b, w_full.T, preferred_element_type=jnp.float32).astype(jnp.bfloat16)
     kappa = 4.0 / jnp.sqrt(jnp.float32(members * total))
     out_term = jnp.dot(cot_b, act, preferred_element_type=jnp.float32)
-    sum_w2, sum_b2, sum_b1, sum_loss = lax.psum(
-        (out_term, jnp.sum(cot, axis=1), jnp.sum(dpre, axis=0), jnp.sum(terms)), ("member", "grid")
+    sum_w2, sum_b2, sum_b1, sum_loss = _direct_chains(
+        (out_term, jnp.sum(cot, axis=1), jnp.sum(dpre, axis=0), jnp.sum(terms))
     )
     row_count = w_in.shape[0]
     full_term = jnp.dot(hidden_in.T, dpre_b, preferred_element_type=jnp.float32)

time: 315 us -> 403 us (1.28)
  waiting for transfers between devices: 202 us -> 299 us
  blocking collectives: 40.3 us -> 27 us
  matrix products: 40.7 us -> 47.5 us
    psum x1, waiting for transfers between devices: 95.1 us -> 146 us  [shards(): summed = lax.psum(full_term, ('member', 'grid'))]
    psum x0 -> x2, waiting for transfers between devices: none -> 45.2 us  [the longest x1 44.6 us: _direct_chains(): now = lax.psum(my_tile, axis_name='grid')]
    psum x1 -> x2, blocking collectives: 40.3 us -> 27 us  [the longest x1 16.2 us: _direct_chains(): now = lax.psum(my_tile, axis_name='grid')]
  transfers between devices with their start and end apart: 3 -> 5, of which waited for: 3 -> 5; matrix products, arithmetic and copies ran while one was open for 3% -> 8% of each run, Pallas kernels for 0% -> 0%
where the time goes in v1:
time: 403 us
  waiting for transfers between devices  299 us (74%)
  matrix products  47.5 us (12%)
  blocking collectives  27 us (7%)
  between operations  15.7 us (4%)
  other arithmetic  10.1 us (3%)
    psum x1, waiting for transfers between devices, shards(): summed = lax.psum(full_term, ('member', 'grid'))  146 us
    all_gather x1, waiting for transfers between devices, shards(): w_full = lax.all_gather(w_in, ('member', 'grid'), axis=0, tiled=True)  62.1 us
    psum x1, waiting for transfers between devices, _direct_chains(): now = lax.psum(my_tile, axis_name='grid')  44.6 us
    all_gather x1, waiting for transfers between devices, shards(): lax.all_gather(field[None], 'member', axis=0, tiled=True)  44.5 us
    psum x1, blocking collectives, _direct_chains(): now = lax.psum(my_tile, axis_name='grid')  16.2 us
    dot_general x1, matrix products, shards(): jnp.dot(hidden_in, w_full, preferred_element_type=jnp.float32)  12.5 us
    psum x1, blocking collectives, _direct_chains(): return lax.psum(now, axis_name='member')  10.8 us
    dot_general x1, matrix products, shards(): dact = jnp.dot(cot_b.T, w_out, preferred_element_type=jnp.float32)  10.1 us
  transfers between devices with their start and end apart: 5, of which 5 were waited for; matrix products, arithmetic and copies ran while one was open for 8% of the time, Pallas kernels for 0%

profile of v1, /device:TPU:0, one launch (start us, length us, event | category | flops | bytes accessed | tf_op | source)
XLA Modules:
  0.0 402.7 jit_solution(18315557388715117522)
XLA Ops:
  7.2 0.0 copy-start
  7.2 0.0 all-gather.5.cloned.1.call-start
  7.2 0.7 all-gather.5.cloned.1.call-update
  7.9 0.0 copy-start.5
  7.9 0.0 all-gather.7.cloned.1.call-start
  8.0 62.1 %all-gather.5.cloned.1.call-done = bf16[1024,1024]{1,0:T(8,128)(2,1)} async-done(((bf16[32,1024]{1,0:T(8,128)(2,1)}), bf16[1024,1024]{1,0:T(8,128)(2,1)}) %all-gather.5.cloned.1.call-update) | async-done | bytes 2097168 | tf_op jit(solution)/shard_map/all_gather | solution.py:33
  70.1 12.5 %multiply_convert_fusion = (bf16[2048,1024]{1,0:T(8,128)(2,1)S(1)}, f32[2048,1024]{1,0:T(8,128)}) fusion(f32[1024]{0:T(1024)} %param.10, bf16[1024,1024]{1,0:T(8,128)(2,1)} %all-gather.5.cloned.1.call-done, bf16[1,2048,1024]{2,1,0:T(8,128)(2,1)} %param.8), kind=kOutput, calls=%fused_computation.8 | convolution fusion | flops 4315938816 | bytes 18878464 | tf_op jit(solution)/shard_map/dot_general | solution.py:43
  82.6 0.0 copy-start.1
  82.6 0.0 copy-start.6
  82.6 2.0 copy-done.1
  84.6 0.0 copy-done
  84.6 0.0 copy-done.5
  84.6 2.4 convolution_add_fusion
  87.0 0.0 all-gather.7.cloned.1.call-update
  87.0 0.2 all-reduce.8.cloned.1.call-start
  87.2 0.0 copy-done.6
  87.2 0.2 dynamic-slice_reduce_fusion
  87.4 0.1 multiply_cosine_fusion
  87.5 0.1 convert_reduce_fusion
  87.6 44.5 %all-gather.7.cloned.1.call-done = f32[4,100,2048]{2,1,0:T(8,128)} async-done(((f32[1,100,2048]{2,1,0:T(8,128)}), f32[4,100,2048]{2,1,0:T(8,128)}) %all-gather.7.cloned.1.call-update) | async-done | bytes 3276816 | tf_op jit(solution)/shard_map/all_gather | solution.py:53
  132.0 3.9 fusion.10
  136.0 0.0 copy-start.3
  136.0 0.0 copy-start.4
  136.0 0.0 copy-start.7
  136.0 1.3 fusion.12
  137.4 0.0 copy-start.2
  137.4 1.3 fusion.14
  138.7 0.0 copy-done.3
  138.7 0.0 copy-done.4
  138.7 0.0 copy-done.7
  138.7 0.0 copy-start.9
  138.8 1.9 fusion.29
  140.6 0.0 copy-done.2
  140.6 1.6 fusion.24
  142.2 0.0 all-reduce.8.cloned.1.call-update
  142.2 0.0 all-reduce.10.cloned.1.call-start
  142.3 0.0 copy-done.9
  142.3 10.1 %fusion.30 = (f32[1024]{0:T(1024)S(1)}, bf16[2048,1024]{1,0:T(8,128)(2,1)}) fusion(f32[2048,1024]{1,0:T(8,128)} %get-tuple-element.36, f32[1024]{0:T(1024)S(1)} %copy-done.9, bf16[100,1024]{1,0:T(8,128)(2,1)S(1)} %copy-done, bf16[100,2048]{1,0:T(8,128)(2,1)S(1)} %get-tuple-element.31), kind=kOutput, calls=%fused_computation.47 | convolution fusion | flops 465566720 | bytes 13205504 | tf_op jit(solution)/shard_map/dot_general | solution.py:61
  152.4 44.6 %all-reduce.8.cloned.1.call-done = f32[100,1024]{1,0:T(8,128)} async-done(((f32[100,1024]{1,0:T(8,128)}), f32[100,1024]{1,0:T(8,128)}) %all-reduce.8.cloned.1.call-update) | async-done | bytes 409616 | tf_op jit(solution)/shard_map/psum | solution.py:27
  196.9 0.0 all-reduce.10.cloned.1.call-update
  197.0 0.3 all-reduce.6.cloned.1.call-start
  197.2 10.0 %fusion.16 = f32[1024,1024]{0,1:T(8,128)} fusion(bf16[1,2048,1024]{2,1,0:T(8,128)(2,1)} %param.8, bf16[2048,1024]{1,0:T(8,128)(2,1)} %get-tuple-element.38), kind=kOutput, calls=%fused_computation.22 | convolution fusion | flops 4294967296 | bytes 12582912 | tf_op jit(solution)/shard_map/dot_general | solution.py:72
  207.2 0.0 copy-start.8
  207.2 0.0 all-reduce.6.cloned.1.call-update
  207.3 16.2 %all-reduce = (f32[]{:T(128)}, f32[1024]{0:T(1024)S(1)}, f32[100]{0:T(128)S(1)}) all-reduce(f32[]{:T(128)} %get-tuple-element.34, f32[1024]{0:T(1024)S(1)} %get-tuple-element.37, f32[100]{0:T(128)S(1)} %get-tuple-element.30), channel_id=1, replica_groups=mesh['member'=4,'grid'=8] {'grid'}, use_global_device_ids=true, to_apply=%region_2.3 | all-reduce | flops 1125 | bytes 9000 | tf_op jit(solution)/shard_map/psum | solution.py:27
  223.4 10.8 %all-reduce.1 = (f32[]{:T(128)}, f32[1024]{0:T(1024)S(1)}, f32[100]{0:T(128)S(1)}) all-reduce(f32[]{:T(128)} %get-tuple-element.24, f32[1024]{0:T(1024)S(1)} %get-tuple-element.25, f32[100]{0:T(128)S(1)} %get-tuple-element.26), channel_id=1, replica_groups=mesh['member'=4,'grid'=8] {'member'}, use_global_device_ids=true, to_apply=%region_3.4 | all-reduce | flops 1125 | bytes 9000 | tf_op jit(solution)/shard_map/psum | solution.py:28
  234.9 0.5 broadcast_multiply_fusion.2
  235.5 0.6 broadcast_multiply_fusion.1
  236.1 0.0 copy-done.8
  236.1 8.3 %convert_bitcast_fusion = bf16[1,2048,1024]{2,1,0:T(8,128)(2,1)} fusion(bf16[1024,1024]{1,0:T(8,128)(2,1)S(1)} %copy-done.8, bf16[2048,1024]{1,0:T(8,128)(2,1)} %get-tuple-element.38), kind=kOutput, calls=%fused_computation.13 | convolution fusion | flops 4297064448 | bytes 10485760 | tf_op jit(solution)/shard_map/dot_general | solution.py:65
  244.4 0.6 all-reduce.10.cloned.1.call-done
  245.0 1.8 broadcast_multiply_fusion
  246.8 146.1 %all-reduce.6.cloned.1.call-done = f32[1024,1024]{0,1:T(8,128)} async-done(((f32[1024,1024]{0,1:T(8,128)}), f32[1024,1024]{0,1:T(8,128)}) %all-reduce.6.cloned.1.call-update) | async-done | bytes 4194320 | tf_op jit(solution)/shard_map/psum | solution.py:73
  392.9 1.2 dynamic-slice_multiply_fusion
  394.2 0.8 copy.16
Async XLA Ops:
  7.2 77.4 %copy-start = (bf16[100,1024]{1,0:T(8,128)(2,1)S(1)}, bf16[100,1024]{1,0:T(8,128)(2,1)}, u32[]{:S(2)}) copy-start(bf16[100,1024]{1,0:T(8,128)(2,1)} %param.11) | copy-start | bytes 614404
  7.2 62.9 %all-gather.5.cloned.1.call-start = ((), (), s32[]{:S(2)}) async-start(), calls=%async_computation | async-start | bytes 2162688 | tf_op jit(solution)/shard_map/all_gather | solution.py:33
  7.9 76.7 %copy-start.5 = (f32[100]{0:T(128)S(1)}, f32[100]{0:T(128)}, u32[]{:S(2)}) copy-start(f32[100]{0:T(128)} %param.12) | copy-start | bytes 1204
  7.9 124.1 %all-gather.7.cloned.1.call-start = ((), (), s32[]{:S(2)}) async-start(), calls=%async_computation.4 | async-start | bytes 4259840 | tf_op jit(solution)/shard_map/all_gather | solution.py:53
  82.6 2.0 copy-start.1
  82.6 4.6 %copy-start.6 = (s32[3,4]{1,0:T(4,128)S(1)}, s32[3,4]{1,0:T(4,128)}, u32[]{:S(2)}) copy-start(s32[3,4]{1,0:T(4,128)} %param.15) | copy-start | bytes 148
  87.0 109.9 %all-reduce.8.cloned.1.call-start = ((), (), s32[]{:S(2)}) async-start(), calls=%async_computation.2 | async-start | bytes 851968 | tf_op jit(solution)/shard_map/psum | solution.py:27
  136.0 2.7 copy-start.3
  136.0 2.7 copy-start.4
  136.0 2.7 copy-start.7
  137.4 3.3 copy-start.2
  138.7 3.5 copy-start.9
  142.2 102.8 %all-reduce.10.cloned.1.call-start = ((), (), s32[]{:S(2)}) async-start(), calls=%async_computation.3 | async-start | bytes 851968 | tf_op jit(solution)/shard_map/psum | solution.py:28
  197.0 196.0 %all-reduce.6.cloned.1.call-start = ((), (), s32[]{:S(2)}) async-start(), calls=%async_computation.1 | async-start | bytes 8388608 | tf_op jit(solution)/shard_map/psum | solution.py:73
  207.2 28.8 %copy-start.8 = (bf16[1024,1024]{1,0:T(8,128)(2,1)S(1)}, bf16[1024,1024]{1,0:T(8,128)(2,1)}, u32[]{:S(2)}) copy-start(bf16[1024,1024]{1,0:T(8,128)(2,1)} %all-gather.5.cloned.1.call-done) | copy-start | bytes 6291460
Sparse Core Ops, SparseCore 0:
  11.0 59.0 all-gather.4
  87.1 44.8 all-gather.6
  142.3 54.5 all-reduce.7
  199.8 45.1 all-reduce.9
  250.4 142.4 all-reduce.5
